TPU v7x, 32 devices: a whole 2x2x4 slice. The times are simulated.
32 devices in a mesh: expert: 4 (over z), dp: 8 (over y, x, core).
Axes of the slice: x: 2, y: 2, z: 4, core: 2. Of those that a mesh axis runs over, the one named last changes fastest.
Arguments:
- tokens: bfloat16 [3072, 2304], P(('expert', 'dp')), may hold values from -6 to 6
- expert_ids: int32 [3072, 2], P(('expert', 'dp')), may hold values from 0 to 3, all different within a row; in each aligned block of 96 rows (0 to 95, 96 to 191, ...) at most 64 rows name the same one
- gate_weights: float32 [3072, 2], P(('expert', 'dp')), may hold values from 0.2 to 1
- request_lengths: int32 [32, 4], P(('expert', 'dp')), may hold values from 1 to 48, 96 in all within a row
- request_adapter: int32 [32, 4], P(('expert', 'dp')), may hold values from 0 to 63
- expert_weights: bfloat16 [4, 2, 2304, 5760], P('expert', None, None, 'dp'), may hold values from -0.125 to 0.125
- expert_down: bfloat16 [4, 5760, 2304], P('expert', 'dp'), may hold values from -0.078125 to 0.078125
- low_down: bfloat16 [4, 2304, 2048], P('expert', None, 'dp'), may hold values from -0.125 to 0.125
- low_up: bfloat16 [4, 2, 1024, 5760], P('expert', None, None, 'dp'), may hold values from -1.5 to 1.5
Outputs:
- mixed: bfloat16 [3072, 2304], P(('expert', 'dp'))
Inputs may be any that keep to these rules, and one draw needn't show every extreme that they name: `expert_ids`: each row names 2 different experts; within the rows of one device no expert is named by more than 64 rows, a bound that some block reaches. `request_lengths`: each row sums to 96, and its largest entry is exactly 48.
All inputs are finite; a program needn't handle non-finite values.
Results may differ from a plain program's by a relative error of at most 0.017.
Values may be sent and summed in bfloat16 or wider, within the bound.
No kernel may reach another device: no remote copies, remote signals or barrier semaphores. Data moves between devices by JAX's collectives and lax.ppermute only.
A program may use at most 192 MiB of HBM per device.

v0:
```python
import jax
import jax.numpy as jnp
from jax import lax
from jax.sharding import PartitionSpec as P

TOP = 2
RANK = 16


def body(
    tokens,
    expert_ids,
    gate_weights,
    request_lengths,
    request_adapter,
    expert_weights,
    expert_down,
    low_down,
    low_up,
):
    ways_expert = lax.axis_size("expert")
    local_tokens = tokens.shape[0]
    width = tokens.shape[1]
    experts_all = ways_expert * expert_down.shape[0]
    capacity = local_tokens * TOP * 4 // (3 * experts_all)
    slots_all = experts_all * capacity
    held = low_down.shape[2] // (2 * RANK)
    adapters_all = low_up.shape[2] // RANK
    values = tokens.astype(jnp.float32)
    normed = (values * lax.rsqrt(jnp.mean(values * values, axis=1, keepdims=True) + 1e-05)).astype(
        jnp.bfloat16
    )
    ends = jnp.cumsum(request_lengths[0])
    place = jnp.arange(local_tokens, dtype=jnp.int32)
    which = jnp.sum((place[:, None] >= ends[None, :]).astype(jnp.int32), axis=1)
    lookup = (
        which[:, None] == jnp.arange(request_lengths.shape[1], dtype=jnp.int32)[None, :]
    ).astype(jnp.int32)
    adapter = jnp.sum(lookup * request_adapter[0][None, :], axis=1)
    flat = expert_ids.reshape(-1)
    onehot = (flat[:, None] == jnp.arange(experts_all, dtype=jnp.int32)[None, :]).astype(jnp.int32)
    slot = jnp.sum((jnp.cumsum(onehot, axis=0) - onehot) * onehot, axis=1)
    target = flat * capacity + slot
    placement_weights = (jnp.arange(slots_all, dtype=jnp.int32)[:, None] == target[None, :]).astype(
        jnp.bfloat16
    )
    pairs = jnp.repeat(normed, TOP, axis=0)
    outgoing = (
        jnp.dot(placement_weights, pairs, preferred_element_type=jnp.float32)
        .astype(jnp.bfloat16)
        .reshape(experts_all, capacity, width)
    )
    pair_adapter = jnp.repeat(adapter, TOP).astype(jnp.float32)
    outgoing_ids = (
        jnp.dot(placement_weights.astype(jnp.float32), pair_adapter)
        .astype(jnp.bfloat16)
        .reshape(experts_all, capacity)
    )
    arrived, arrived_ids = (
        lax.all_to_all(outgoing, "expert", split_axis=0, concat_axis=0, tiled=True),
        lax.all_to_all(outgoing_ids, "expert", split_axis=0, concat_axis=0, tiled=True),
    )
    rows, labels_wire = (
        lax.all_gather(arrived.reshape(-1, width), "dp", axis=0, tiled=True),
        lax.all_gather(arrived_ids.reshape(-1), "dp", axis=0, tiled=True),
    )
    rows_total = rows.shape[0]
    labels = labels_wire.astype(jnp.int32)
    group = lax.axis_index("dp")
    projected = jnp.dot(rows, low_down[0], preferred_element_type=jnp.float32).reshape(
        rows_total, held, 2 * RANK
    )
    owned = (labels[:, None] == group * held + jnp.arange(held, dtype=jnp.int32)[None, :]).astype(
        jnp.float32
    )
    lowrank_part = jnp.sum(owned[:, :, None] * projected, axis=1)
    lowrank = lax.psum(lowrank_part.astype(jnp.bfloat16), "dp")
    marks = (labels[:, None] == jnp.arange(adapters_all, dtype=jnp.int32)[None, :]).astype(
        jnp.bfloat16
    )
    spread_gate = (marks[:, :, None] * lowrank[:, None, :RANK]).reshape(
        lax.axis_size("dp") * (ways_expert * capacity), adapters_all * RANK
    )
    sharded_up_weight = (marks[:, :, None] * lowrank[:, None, RANK:]).reshape(
        lax.axis_size("dp") * (ways_expert * capacity), adapters_all * RANK
    )
    gate = jnp.dot(rows, expert_weights[0, 0], preferred_element_type=jnp.float32) + jnp.dot(
        spread_gate, low_up[0, 0], preferred_element_type=jnp.float32
    )
    up = jnp.dot(rows, expert_weights[0, 1], preferred_element_type=jnp.float32) + jnp.dot(
        sharded_up_weight, low_up[0, 1], preferred_element_type=jnp.float32
    )
    hidden_activations = (jax.nn.silu(gate) * up).astype(jnp.bfloat16)
    mine = lax.psum_scatter(
        jnp.dot(hidden_activations, expert_down[0], preferred_element_type=jnp.float32).astype(
            jnp.bfloat16
        ),
        "dp",
        scatter_dimension=0,
        tiled=True,
    ).astype(jnp.float32)
    mine = mine.astype(jnp.bfloat16).reshape(ways_expert, capacity, width)
    back = lax.all_to_all(mine, "expert", split_axis=0, concat_axis=0, tiled=True)
    picked = jnp.dot(
        placement_weights.T, back.reshape(slots_all, width), preferred_element_type=jnp.float32
    ).reshape(local_tokens, TOP, width)
    mixed = values + jnp.sum(gate_weights[:, :, None] * picked, axis=1)
    return mixed.astype(jnp.bfloat16)


def solution(mesh):
    return jax.shard_map(
        body,
        mesh=mesh,
        in_specs=(
            P(("expert", "dp"), None),
            P(("expert", "dp"), None),
            P(("expert", "dp"), None),
            P(("expert", "dp"), None),
            P(("expert", "dp"), None),
            P("expert", None, None, "dp"),
            P("expert", "dp", None),
            P("expert", None, "dp"),
            P("expert", None, None, "dp"),
        ),
        out_specs=P(("expert", "dp"), None),
        check_vma=False,
    )
```

profile of v0, /device:TPU:0, one launch (start us, length us, event | category | flops | bytes accessed | tf_op | source)
XLA Modules:
  0.0 319.4 jit_solution(102362111478720045)
XLA Ops:
  6.5 0.9 copy.24
  7.6 1.2 reduce-window.18
  9.3 1.2 fusion.24
  10.5 1.2 fusion.25
  11.7 1.4 broadcast_in_dim.4
  13.1 3.1 reshape.195
  16.2 1.6 convolution_convert_fusion.1
  17.9 34.8 %all_to_all.20 = bf16[4,64,2304]{2,1,0:T(8,128)(2,1)} all-to-all(bf16[4,64,2304]{2,1,0:T(8,128)(2,1)S(1)} %bitcast.58), channel_id=1, replica_groups=mesh['expert'=4,'dp'=8] {'expert'}, dimensions={0} | all-to-all | bytes 2359296 | tf_op jit(solution)/shard_map/all_to_all | solution.py:60
  52.7 0.2 reduce-window.20
  53.1 0.2 reshape.208
  53.3 0.2 fusion.28
  53.4 0.7 all_to_all.16
  54.1 3.2 %all-to-all-start.1 = ((bf16[4,1,64]{2,1,0:T(2,128)(2,1)}), bf16[4,1,64]{2,1,0:T(2,128)(2,1)S(1)}, u32[]{:S(2)}, u32[]{:S(2)}) async-start(bf16[4,1,64]{2,1,0:T(2,128)(2,1)} %all_to_all.16), calls=%async_computation.1 | async-start | bytes 4096 | tf_op jit(solution)/shard_map/all_to_all | solution.py:61
  57.4 2.4 copy.28
  59.9 2.9 all-to-all-done.1
  62.9 8.9 %all-gather = bf16[8,1,256]{2,1,0:T(2,128)(2,1)S(1)} all-gather(bf16[1,1,256]{2,1,0:T(2,128)(2,1)S(1)} %reshape.204), channel_id=1, replica_groups=mesh['expert'=4,'dp'=8] {'dp'}, dimensions={0}, use_global_device_ids=true | all-gather | bytes 4608 | tf_op jit(solution)/shard_map/all_gather | solution.py:65
  71.9 0.8 fusion.27
  72.6 38.1 %all-gather.3.cloned.1.call-done = bf16[2048,2304]{1,0:T(8,128)(2,1)} async-done(((bf16[256,2304]{1,0:T(8,128)(2,1)}), bf16[2048,2304]{1,0:T(8,128)(2,1)}) %all-gather.3.cloned.1.call-update) | async-done | bytes 9437200 | tf_op jit(solution)/shard_map/all_gather | solution.py:64
  110.8 7.3 %fusion.21 = bf16[2048,32]{0,1:T(8,128)(2,1)} fusion(bf16[8,32,2304]{2,1,0:T(8,128)(2,1)} %bitcast.62, bf16[2048,2304]{1,0:T(8,128)(2,1)} %all-gather.3.cloned.1.call-done, f32[2048,8]{0,1:T(8,128)S(1)} %compare_convert_fusion), kind=kOutput, calls=%fused_computation.23 | convolution fusion | flops 2416902144 | bytes 10813440 | tf_op jit(solution)/shard_map/dot_general | solution.py:70
  118.1 0.2 reduce-scatter.2.cloned.1.call-start
  118.3 12.2 %fusion.3 = f32[2048,720]{0,1:T(8,128)} fusion(bf16[2048,2304]{1,0:T(8,128)(2,1)} %all-gather.3.cloned.1.call-done, bf16[1,2,2304,720]{2,3,1,0:T(8,128)(2,1)} %param.14), kind=kOutput, calls=%fused_computation.7 | convolution fusion | flops 6794772480 | bytes 18653184 | tf_op jit(solution)/shard_map/dot_general | solution.py:90
  130.5 12.2 %fusion.5 = f32[2048,720]{0,1:T(8,128)} fusion(bf16[2048,2304]{1,0:T(8,128)(2,1)} %all-gather.3.cloned.1.call-done, bf16[1,2,2304,720]{2,3,1,0:T(8,128)(2,1)} %param.14), kind=kOutput, calls=%fused_computation.9 | convolution fusion | flops 6794772480 | bytes 18653184 | tf_op jit(solution)/shard_map/dot_general | solution.py:87
  142.8 28.4 %all-reduce.3.cloned.1.call-done = bf16[2048,32]{0,1:T(8,128)(2,1)} async-done(((bf16[2048,32]{0,1:T(8,128)(2,1)}), bf16[2048,32]{0,1:T(8,128)(2,1)}) %all-reduce.3.cloned.1.call-update) | async-done | bytes 131088 | tf_op jit(solution)/shard_map/psum | solution.py:77
  171.2 0.9 fusion.35
  172.1 3.7 %broadcast_multiply_fusion = (bf16[2048,64,16]{0,2,1:T(8,128)(2,1)}, bf16[2048,64,16]{0,2,1:T(8,128)(2,1)S(1)}) fusion(bf16[2048,16]{0,1:T(8,128)(2,1)S(1)} %get-tuple-element.7, bf16[2048,64]{0,1:T(8,128)(2,1)} %fusion.27, bf16[2048,16]{0,1:T(8,128)(2,1)S(1)} %get-tuple-element.8), kind=kLoop, calls=%fused_computation.15 | loop fusion | flops 4194304 | bytes 8781824 | tf_op jit(solution)/shard_map/mul | solution.py:84
  175.8 5.2 %fusion.15 = f32[2048,720]{0,1:T(8,128)} fusion(bf16[2048,1024]{0,1:T(8,128)(2,1)S(1)} %bitcast.61, bf16[1,2,1024,720]{2,3,1,0:T(8,128)(2,1)S(1)} %copy-done.2), kind=kOutput, calls=%fused_computation.18 | convolution fusion | flops 3019898880 | bytes 11567104 | tf_op jit(solution)/shard_map/dot_general | solution.py:87
  181.0 18.9 %convolution_convert_fusion = bf16[2048,2304]{1,0:T(8,128)(2,1)} fusion(bf16[1,720,2304]{2,1,0:T(8,128)(2,1)S(1)} %copy-done, f32[2048,720]{0,1:T(8,128)} %fusion.3, f32[2048,720]{0,1:T(8,128)} %fusion.5, f32[2048,720]{0,1:T(8,128)} %fusion.15, bf16[2048,1024]{0,1:T(8,128)(2,1)} %bitcast.60, bf16[1,2,1024,720]{2,3,1,0:T(8,128)(2,1)} %param.17), kind=kOutput, calls=%fused_computation | convolution fusion | flops 9831186432 | bytes 36118528 | tf_op jit(solution)/shard_map/dot_general | solution.py:95
  199.9 76.0 %reduce-scatter.2.cloned.1.call-done = bf16[256,2304]{1,0:T(8,128)(2,1)} async-done(((bf16[2048,2304]{1,0:T(8,128)(2,1)}), bf16[256,2304]{1,0:T(8,128)(2,1)}) %reduce-scatter.2.cloned.1.call-update) | async-done | bytes 1179664 | tf_op jit(solution)/shard_map/reduce_scatter | solution.py:94
  276.0 4.6 %all-to-all-start.2 = ((bf16[4,64,2304]{2,1,0:T(8,128)(2,1)}), bf16[4,64,2304]{2,1,0:T(8,128)(2,1)}, u32[]{:S(2)}, u32[]{:S(2)}) async-start(bf16[4,64,2304]{2,1,0:T(8,128)(2,1)} %bitcast.63), calls=%async_computation.3 | async-start | bytes 2359296 | tf_op jit(solution)/shard_map/all_to_all | solution.py:103
  280.7 28.5 %all-to-all-done.2 = bf16[4,64,2304]{2,1,0:T(8,128)(2,1)} async-done(((bf16[4,64,2304]{2,1,0:T(8,128)(2,1)}), bf16[4,64,2304]{2,1,0:T(8,128)(2,1)}, u32[]{:S(2)}, u32[]{:S(2)}) %all-to-all-start.2) | async-done | bytes 1179680 | tf_op jit(solution)/shard_map/all_to_all | solution.py:103
  309.2 1.7 fusion.20
  311.0 1.9 fusion.26
  (41 shorter events, 1.3 us)
Async XLA Ops:
  6.5 174.4 %copy-start = (bf16[1,720,2304]{2,1,0:T(8,128)(2,1)S(1)}, bf16[1,720,2304]{2,1,0:T(8,128)(2,1)}, u32[]{:S(2)}) copy-start(bf16[1,720,2304]{2,1,0:T(8,128)(2,1)} %param.15) | copy-start | bytes 9953284
  6.5 104.2 %all-gather.3.cloned.1.call-start = ((), (), s32[]{:S(2)}) async-start(), calls=%async_computation.4 | async-start | bytes 10616832 | tf_op jit(solution)/shard_map/all_gather | solution.py:64
  11.7 41.0 %copy-start.3 = (s32[1,4]{1,0:T(1,128)S(1)}, s32[1,4]{1,0:T(1,128)}, u32[]{:S(2)}) copy-start(s32[1,4]{1,0:T(1,128)} %param.12) | copy-start | bytes 52
  11.7 41.2 %copy-start.4 = (s32[1,4]{1,0:T(1,128)S(1)}, s32[1,4]{1,0:T(1,128)}, u32[]{:S(2)}) copy-start(s32[1,4]{1,0:T(1,128)} %param.13) | copy-start | bytes 52
  54.1 8.7 %all-to-all-start.1 = ((bf16[4,1,64]{2,1,0:T(2,128)(2,1)}), bf16[4,1,64]{2,1,0:T(2,128)(2,1)S(1)}, u32[]{:S(2)}, u32[]{:S(2)}) async-start(bf16[4,1,64]{2,1,0:T(2,128)(2,1)} %all_to_all.16), calls=%async_computation.1 | async-start | bytes 4096 | tf_op jit(solution)/shard_map/all_to_all | solution.py:61
  57.4 113.8 %all-reduce.3.cloned.1.call-start = ((), (), s32[]{:S(2)}) async-start(), calls=%async_computation.5 | async-start | bytes 262144 | tf_op jit(solution)/shard_map/psum | solution.py:77
  118.1 157.9 %reduce-scatter.2.cloned.1.call-start = ((), (), s32[]{:S(2)}) async-start(), calls=%async_computation.6 | async-start | bytes 10616832 | tf_op jit(solution)/shard_map/reduce_scatter | solution.py:94
  172.1 3.7 %copy-start.2 = (bf16[1,2,1024,720]{2,3,1,0:T(8,128)(2,1)S(1)}, bf16[1,2,1024,720]{2,3,1,0:T(8,128)(2,1)}, u32[]{:S(2)}) copy-start(bf16[1,2,1024,720]{2,3,1,0:T(8,128)(2,1)} %param.17) | copy-start | bytes 8847364
  199.9 109.3 %copy-start.1 = (f32[96,2]{0,1:T(2,128)S(1)}, f32[96,2]{0,1:T(2,128)}, u32[]{:S(2)}) copy-start(f32[96,2]{0,1:T(2,128)} %param.11) | copy-start | bytes 2308
  276.0 33.2 %all-to-all-start.2 = ((bf16[4,64,2304]{2,1,0:T(8,128)(2,1)}), bf16[4,64,2304]{2,1,0:T(8,128)(2,1)}, u32[]{:S(2)}, u32[]{:S(2)}) async-start(bf16[4,64,2304]{2,1,0:T(8,128)(2,1)} %bitcast.63), calls=%async_computation.3 | async-start | bytes 2359296 | tf_op jit(solution)/shard_map/all_to_all | solution.py:103
Sparse Core Ops, SparseCore 0:
  52.8 57.9 all-gather.2
  118.2 52.9 all-reduce.2
  200.1 75.8 reduce-scatter.1
where the time goes:
time: 320 us; the launch traced here: 319 us
  waiting for transfers between devices  174 us (54%)
  matrix products  59.4 us (19%)
  blocking collectives  43.7 us (14%)
  between operations  13.3 us (4%)
  other arithmetic  10.7 us (3%)
  local copies, waits for them, and re-layouts  10.3 us (3%)
  starting transfers between devices  8.09 us (3%)
    reduce_scatter x1, waiting for transfers between devices, body(): lax.psum_scatter(jnp.dot(hidden_activations, expert_down[0], preferred_el...  76 us
    all_gather x1, waiting for transfers between devices, body(): lax.all_gather(arrived.reshape(-1, width), 'dp', axis=0, tiled=True)  38.1 us
    all_to_all x1, blocking collectives, body(): lax.all_to_all(outgoing, 'expert', split_axis=0, concat_axis=0, tiled=True)  34.8 us
    all_to_all x1, waiting for transfers between devices, body(): lax.all_to_all(mine, 'expert', split_axis=0, concat_axis=0, tiled=True)  28.5 us
    psum x1, waiting for transfers between devices, body(): lowrank = lax.psum(lowrank_part.astype(jnp.bfloat16), 'dp')  28.4 us
    dot_general x1, matrix products, body(): jnp.dot(hidden_activations, expert_down[0], preferred_element_type=jnp.fl...  18.9 us
    dot_general x1, matrix products, body(): jnp.dot(rows, expert_weights[0, 0], preferred_element_type=jnp.float32)  12.2 us
    dot_general x1, matrix products, body(): jnp.dot(rows, expert_weights[0, 1], preferred_element_type=jnp.float32)  12.2 us
  transfers between devices with their start and end apart: 5, of which 5 were waited for; matrix products, arithmetic and copies ran while one was open for 9% of the time, Pallas kernels for 0%

commit v1 on v0

--- a/solution.py
+++ b/solution.py
@@ -5,6 +5,10 @@
 
 TOP = 2
 RANK = 16
+
+
+def end_points(my_data, axis_key):
+    return jnp.sum(jax.lax.all_gather(my_data, axis_key), axis=0)
 
 
 def body(
@@ -74,7 +78,7 @@
         jnp.float32
     )
     lowrank_part = jnp.sum(owned[:, :, None] * projected, axis=1)
-    lowrank = lax.psum(lowrank_part.astype(jnp.bfloat16), "dp")
+    lowrank = end_points(lowrank_part.astype(jnp.bfloat16), "dp")
     marks = (labels[:, None] == jnp.arange(adapters_all, dtype=jnp.int32)[None, :]).astype(
         jnp.bfloat16
     )

time: 320 us -> 294 us (0.919)
  waiting for transfers between devices: 174 us -> 146 us
    psum x1 -> x0, waiting for transfers between devices: 28.4 us -> none  [body(): lowrank = lax.psum(lowrank_part.astype(jnp.bfloat16), 'dp')]
  transfers between devices with their start and end apart: 5 -> 5, of which waited for: 5 -> 4; matrix products, arithmetic and copies ran while one was open for 9% -> 10% of each run, Pallas kernels for 0% -> 0%
where the time goes in v1:
time: 294 us; the launch traced here: 293 us
  waiting for transfers between devices  146 us (50%)
  matrix products  59.6 us (20%)
  blocking collectives  43.7 us (15%)
  between operations  13.3 us (5%)
  other arithmetic  11.4 us (4%)
  local copies, waits for them, and re-layouts  11.2 us (4%)
  starting transfers between devices  8.06 us (3%)
    reduce_scatter x1, waiting for transfers between devices, body(): lax.psum_scatter(jnp.dot(hidden_activations, expert_down[0], preferred_el...  76.7 us
    all_gather x1, waiting for transfers between devices, body(): lax.all_gather(arrived.reshape(-1, width), 'dp', axis=0, tiled=True)  38.1 us
    all_to_all x1, blocking collectives, body(): lax.all_to_all(outgoing, 'expert', split_axis=0, concat_axis=0, tiled=True)  34.8 us
    all_to_all x1, waiting for transfers between devices, body(): lax.all_to_all(mine, 'expert', split_axis=0, concat_axis=0, tiled=True)  28.5 us
    dot_general x1, matrix products, body(): jnp.dot(hidden_activations, expert_down[0], preferred_element_type=jnp.fl...  19.2 us
    dot_general x1, matrix products, body(): jnp.dot(rows, expert_weights[0, 0], preferred_element_type=jnp.float32)  12.2 us
    dot_general x1, matrix products, body(): jnp.dot(rows, expert_weights[0, 1], preferred_element_type=jnp.float32)  12.2 us
    all_gather x1, blocking collectives, body(): lax.all_gather(arrived_ids.reshape(-1), 'dp', axis=0, tiled=True)  8.9 us
  transfers between devices with their start and end apart: 5, of which 4 were waited for; matrix products, arithmetic and copies ran while one was open for 10% of the time, Pallas kernels for 0%

profile of v1, /device:TPU:0, one launch (start us, length us, event | category | flops | bytes accessed | tf_op | source)
XLA Modules:
  0.0 293.5 jit_solution(11929419180505860142)
XLA Ops:
  6.5 0.9 copy.24
  7.6 1.2 reduce-window.18
  9.3 1.2 fusion.24
  10.5 1.2 fusion.25
  11.7 1.4 broadcast_in_dim.4
  13.1 3.1 %reshape.203 = bf16[192,2304]{1,0:T(8,128)(2,1)} reshape(bf16[96,2,2304]{2,1,0:T(2,128)(2,1)} %broadcast_in_dim.4) | data formatting | bytes 1769472 | tf_op jit(solution)/shard_map/reshape | solution.py:51
  16.2 1.6 convolution_convert_fusion.1
  17.9 34.8 %all_to_all.20 = bf16[4,64,2304]{2,1,0:T(8,128)(2,1)} all-to-all(bf16[4,64,2304]{2,1,0:T(8,128)(2,1)S(1)} %bitcast.63), channel_id=1, replica_groups=mesh['expert'=4,'dp'=8] {'expert'}, dimensions={0} | all-to-all | bytes 2359296 | tf_op jit(solution)/shard_map/all_to_all | solution.py:64
  52.7 0.2 reduce-window.20
  53.1 0.2 reshape.217
  53.3 0.2 fusion.28
  53.4 0.7 all_to_all.16
  54.1 3.2 %all-to-all-start.1 = ((bf16[4,1,64]{2,1,0:T(2,128)(2,1)}), bf16[4,1,64]{2,1,0:T(2,128)(2,1)S(1)}, u32[]{:S(2)}, u32[]{:S(2)}) async-start(bf16[4,1,64]{2,1,0:T(2,128)(2,1)} %all_to_all.16), calls=%async_computation.1 | async-start | bytes 4096 | tf_op jit(solution)/shard_map/all_to_all | solution.py:65
  57.4 2.4 copy.28
  59.9 2.9 all-to-all-done.1
  62.9 8.9 %all-gather.1 = bf16[8,1,256]{2,1,0:T(2,128)(2,1)S(1)} all-gather(bf16[1,1,256]{2,1,0:T(2,128)(2,1)S(1)} %reshape.213), channel_id=1, replica_groups=mesh['expert'=4,'dp'=8] {'dp'}, dimensions={0}, use_global_device_ids=true | all-gather | bytes 4608 | tf_op jit(solution)/shard_map/all_gather | solution.py:69
  71.9 0.8 fusion.27
  72.6 38.1 %all-gather.5.cloned.1.call-done = bf16[2048,2304]{1,0:T(8,128)(2,1)} async-done(((bf16[256,2304]{1,0:T(8,128)(2,1)}), bf16[2048,2304]{1,0:T(8,128)(2,1)}) %all-gather.5.cloned.1.call-update) | async-done | bytes 9437200 | tf_op jit(solution)/shard_map/all_gather | solution.py:68
  110.8 7.3 %fusion.21 = bf16[2048,32]{0,1:T(8,128)(2,1)} fusion(bf16[8,32,2304]{2,1,0:T(8,128)(2,1)} %bitcast.67, bf16[2048,2304]{1,0:T(8,128)(2,1)} %all-gather.5.cloned.1.call-done, f32[2048,8]{0,1:T(8,128)S(1)} %compare_convert_fusion), kind=kOutput, calls=%fused_computation.23 | convolution fusion | flops 2416902144 | bytes 10813440 | tf_op jit(solution)/shard_map/dot_general | solution.py:74
  118.1 0.2 reduce-scatter.2.cloned.1.call-start
  118.3 12.2 %fusion.3 = f32[2048,720]{0,1:T(8,128)} fusion(bf16[2048,2304]{1,0:T(8,128)(2,1)} %all-gather.5.cloned.1.call-done, bf16[1,2,2304,720]{2,3,1,0:T(8,128)(2,1)} %param.14), kind=kOutput, calls=%fused_computation.7 | convolution fusion | flops 6794772480 | bytes 18653184 | tf_op jit(solution)/shard_map/dot_general | solution.py:94
  130.5 12.2 %fusion.5 = f32[2048,720]{0,1:T(8,128)} fusion(bf16[2048,2304]{1,0:T(8,128)(2,1)} %all-gather.5.cloned.1.call-done, bf16[1,2,2304,720]{2,3,1,0:T(8,128)(2,1)} %param.14), kind=kOutput, calls=%fused_computation.9 | convolution fusion | flops 6794772480 | bytes 18653184 | tf_op jit(solution)/shard_map/dot_general | solution.py:91
  142.7 1.8 copy.31
  144.6 0.8 bitcast_reduce_fusion
  145.4 3.7 %broadcast_multiply_fusion = (bf16[2048,64,16]{0,2,1:T(8,128)(2,1)}, bf16[2048,64,16]{0,2,1:T(8,128)(2,1)S(1)}) fusion(bf16[2048,16]{0,1:T(8,128)(2,1)S(1)} %get-tuple-element.7, bf16[2048,64]{0,1:T(8,128)(2,1)} %fusion.27, bf16[2048,16]{0,1:T(8,128)(2,1)S(1)} %get-tuple-element.8), kind=kLoop, calls=%fused_computation.15 | loop fusion | flops 4194304 | bytes 8781824 | tf_op jit(solution)/shard_map/mul | solution.py:88
  149.1 5.2 %fusion.15 = f32[2048,720]{0,1:T(8,128)} fusion(bf16[2048,1024]{0,1:T(8,128)(2,1)S(1)} %bitcast.66, bf16[1,2,1024,720]{2,3,1,0:T(8,128)(2,1)S(1)} %copy-done.2), kind=kOutput, calls=%fused_computation.18 | convolution fusion | flops 3019898880 | bytes 11567104 | tf_op jit(solution)/shard_map/dot_general | solution.py:91
  154.3 19.2 %convolution_convert_fusion = bf16[2048,2304]{1,0:T(8,128)(2,1)} fusion(bf16[1,720,2304]{2,1,0:T(8,128)(2,1)S(1)} %copy-done, f32[2048,720]{0,1:T(8,128)} %fusion.3, f32[2048,720]{0,1:T(8,128)} %fusion.5, f32[2048,720]{0,1:T(8,128)} %fusion.15, bf16[2048,1024]{0,1:T(8,128)(2,1)} %bitcast.65, bf16[1,2,1024,720]{2,3,1,0:T(8,128)(2,1)} %param.17), kind=kOutput, calls=%fused_computation | convolution fusion | flops 9831186432 | bytes 36118528 | tf_op jit(solution)/shard_map/dot_general | solution.py:99
  173.4 76.7 %reduce-scatter.2.cloned.1.call-done = bf16[256,2304]{1,0:T(8,128)(2,1)} async-done(((bf16[2048,2304]{1,0:T(8,128)(2,1)}), bf16[256,2304]{1,0:T(8,128)(2,1)}) %reduce-scatter.2.cloned.1.call-update) | async-done | bytes 1179664 | tf_op jit(solution)/shard_map/reduce_scatter | solution.py:98
  250.1 4.6 %all-to-all-start.2 = ((bf16[4,64,2304]{2,1,0:T(8,128)(2,1)}), bf16[4,64,2304]{2,1,0:T(8,128)(2,1)}, u32[]{:S(2)}, u32[]{:S(2)}) async-start(bf16[4,64,2304]{2,1,0:T(8,128)(2,1)} %bitcast.68), calls=%async_computation.3 | async-start | bytes 2359296 | tf_op jit(solution)/shard_map/all_to_all | solution.py:107
  254.8 28.5 %all-to-all-done.2 = bf16[4,64,2304]{2,1,0:T(8,128)(2,1)} async-done(((bf16[4,64,2304]{2,1,0:T(8,128)(2,1)}), bf16[4,64,2304]{2,1,0:T(8,128)(2,1)}, u32[]{:S(2)}, u32[]{:S(2)}) %all-to-all-start.2) | async-done | bytes 1179680 | tf_op jit(solution)/shard_map/all_to_all | solution.py:107
  283.3 1.7 fusion.20
  285.1 1.9 fusion.26
  (43 shorter events, 1.3 us)
Async XLA Ops:
  6.5 147.7 %copy-start = (bf16[1,720,2304]{2,1,0:T(8,128)(2,1)S(1)}, bf16[1,720,2304]{2,1,0:T(8,128)(2,1)}, u32[]{:S(2)}) copy-start(bf16[1,720,2304]{2,1,0:T(8,128)(2,1)} %param.15) | copy-start | bytes 9953284
  6.5 104.2 %all-gather.5.cloned.1.call-start = ((), (), s32[]{:S(2)}) async-start(), calls=%async_computation.4 | async-start | bytes 10616832 | tf_op jit(solution)/shard_map/all_gather | solution.py:68
  11.7 41.0 %copy-start.3 = (s32[1,4]{1,0:T(1,128)S(1)}, s32[1,4]{1,0:T(1,128)}, u32[]{:S(2)}) copy-start(s32[1,4]{1,0:T(1,128)} %param.12) | copy-start | bytes 52
  11.7 41.2 %copy-start.4 = (s32[1,4]{1,0:T(1,128)S(1)}, s32[1,4]{1,0:T(1,128)}, u32[]{:S(2)}) copy-start(s32[1,4]{1,0:T(1,128)} %param.13) | copy-start | bytes 52
  54.1 8.7 %all-to-all-start.1 = ((bf16[4,1,64]{2,1,0:T(2,128)(2,1)}), bf16[4,1,64]{2,1,0:T(2,128)(2,1)S(1)}, u32[]{:S(2)}, u32[]{:S(2)}) async-start(bf16[4,1,64]{2,1,0:T(2,128)(2,1)} %all_to_all.16), calls=%async_computation.1 | async-start | bytes 4096 | tf_op jit(solution)/shard_map/all_to_all | solution.py:65
  57.4 85.4 %all-gather.7.cloned.1.call-start = ((), (), s32[]{:S(2)}) async-start(), calls=%async_computation.6 | async-start | bytes 1179648 | tf_op jit(solution)/shard_map/all_gather | solution.py:11
  118.1 132.0 %reduce-scatter.2.cloned.1.call-start = ((), (), s32[]{:S(2)}) async-start(), calls=%async_computation.5 | async-start | bytes 10616832 | tf_op jit(solution)/shard_map/reduce_scatter | solution.py:98
  145.4 3.7 %copy-start.2 = (bf16[1,2,1024,720]{2,3,1,0:T(8,128)(2,1)S(1)}, bf16[1,2,1024,720]{2,3,1,0:T(8,128)(2,1)}, u32[]{:S(2)}) copy-start(bf16[1,2,1024,720]{2,3,1,0:T(8,128)(2,1)} %param.17) | copy-start | bytes 8847364
  173.4 109.9 %copy-start.1 = (f32[96,2]{0,1:T(2,128)S(1)}, f32[96,2]{0,1:T(2,128)}, u32[]{:S(2)}) copy-start(f32[96,2]{0,1:T(2,128)} %param.11) | copy-start | bytes 2308
  250.1 33.2 %all-to-all-start.2 = ((bf16[4,64,2304]{2,1,0:T(8,128)(2,1)}), bf16[4,64,2304]{2,1,0:T(8,128)(2,1)}, u32[]{:S(2)}, u32[]{:S(2)}) async-start(bf16[4,64,2304]{2,1,0:T(8,128)(2,1)} %bitcast.68), calls=%async_computation.3 | async-start | bytes 2359296 | tf_op jit(solution)/shard_map/all_to_all | solution.py:107
Sparse Core Ops, SparseCore 0:
  52.8 57.9 all-gather.4
  118.2 23.4 all-gather.6
  173.6 76.4 reduce-scatter.1
